TPU v7x, 32 devices: a whole 2x2x4 slice. The times are simulated.
32 devices in a mesh: ctx: 16 (over z, x, core), head: 2 (over y).
Axes of the slice: x: 2, y: 2, z: 4, core: 2. Of those that a mesh axis runs over, the one named last changes fastest.
Arguments:
- queries: bfloat16 [2, 16384, 128], P('head', 'ctx'), may hold values from -12 to 12
- key_rows: bfloat16 [2, 16384, 128], P('head', 'ctx'), may hold values from -12 to 12
- value_rows: bfloat16 [2, 16384, 128], P('head', 'ctx'), may hold values from -6 to 6
- cluster_ids: int32 [2, 16384, 1], P('head', 'ctx'), may hold values from 0 to 31; in each aligned block of 1024 rows (0 to 1023, 1024 to 2047, ..., all dimensions but the last counted through in order) at most 64 rows name the same one
- out_weight: bfloat16 [256, 2048], P(None, 'head'), may hold values from -0.375 to 0.375
Outputs:
- projected: bfloat16 [16384, 2048], P('ctx', 'head')
- centroids: float32 [2, 32, 128], P('head', 'ctx')
Inputs may be any that keep to these rules, and one draw needn't show every extreme that they name: `cluster_ids`: in each head, the 1024 tokens of one index of ctx name no cluster more than 64 times, a bound that some block reaches.
All inputs are finite; a program needn't handle non-finite values.
Results may differ from a plain program's by a relative error of at most 0.0054.
Values may be sent and summed in bfloat16 or wider, within the bound.
A program may use at most 64 MiB of HBM per device.

v0:
```python
import math

import jax
import jax.numpy as jnp
from jax import lax
from jax.sharding import PartitionSpec as P

CL_DEV = 2
CAP = 1024


norm_eps = 1e-06


def ranks_of(group):
    length = group.shape[0]
    block = math.gcd(512, length)
    columns = jnp.arange(length, dtype=jnp.int32)

    def block_ranks(start):
        mine = lax.dynamic_slice_in_dim(group, start, block)
        positions = start + jnp.arange(block, dtype=jnp.int32)
        earlier = (mine[:, None] == group[None, :]) & (columns[None, :] < positions[:, None])
        return jnp.sum(earlier.astype(jnp.int32), axis=1)

    starts = jnp.arange(length // block, dtype=jnp.int32) * block
    return lax.map(block_ranks, starts).reshape(length)


def unit_rows(values):
    values = values.astype(jnp.float32)
    return values * lax.rsqrt(jnp.mean(values * values, axis=-1, keepdims=True) + norm_eps)


def cluster_attention(block_q, block_k, block_v, valid):
    length = block_q.shape[0]
    scores = lax.dot_general(
        block_q, block_k, (((1,), (1,)), ((), ())), preferred_element_type=jnp.float32
    )
    scores = scores * jnp.float32(block_q.shape[1] ** (-0.5))
    slots = jnp.arange(length, dtype=jnp.int32)
    allowed = (slots[None, :] <= slots[:, None]) & (
        (valid[None, :] > 0) | (slots[None, :] == slots[:, None])
    )
    scores = jnp.where(allowed, scores, jnp.float32(-1e30))
    highest = jnp.max(scores, axis=1, keepdims=True)
    weights = jnp.exp(scores - highest)
    total = jnp.sum(weights, axis=1, keepdims=True)
    mixed = jnp.dot(weights.astype(jnp.bfloat16), block_v, preferred_element_type=jnp.float32)
    return (mixed / total).astype(jnp.bfloat16)


def attend(q_in, k_in, v_in, counts_in):
    devices, items, send, width = q_in.shape

    def regroup(values):
        return jnp.moveaxis(values, 1, 0).reshape(items, devices * send, width)

    slot_rank = jnp.arange(send, dtype=jnp.int32)
    valid = (slot_rank[None, None, :] < jnp.moveaxis(counts_in, 1, 0)[:, :, None]).astype(jnp.int32)
    valid = valid.reshape(items, devices * send)

    def one_cluster(pieces):
        return cluster_attention(pieces[0], pieces[1], pieces[2], pieces[3])

    attended = lax.map(one_cluster, (regroup(q_in), regroup(k_in), regroup(v_in), valid))
    return jnp.moveaxis(attended.reshape(items, devices, send, width), 0, 1)


def owner_sums(q_in, k_in, counts_in):
    send = q_in.shape[2]
    slot_rank = jnp.arange(send, dtype=jnp.int32)
    valid = slot_rank[None, None, :] < counts_in[:, :, None]
    unit = unit_rows(q_in) + unit_rows(k_in)
    return jnp.sum(jnp.where(valid[:, :, :, None], unit, 0.0), axis=(0, 2))


def shards(queries, key_rows, value_rows, cluster_ids, out_weight):
    group = cluster_ids[0, :, 0]
    length = group.shape[0]
    width = queries.shape[2]
    devices = lax.axis_size("ctx")
    send = CAP // devices
    clusters = CL_DEV * devices
    rank = ranks_of(group)
    where_row = group * send + rank

    def placed_rows(values):
        buffer = jnp.zeros((clusters * send, width), values.dtype).at[where_row].set(values)
        return buffer.reshape(devices, CL_DEV, send, width)

    ones = jnp.ones((length,), jnp.int32)
    counts = jax.ops.segment_sum(ones, group, num_segments=clusters).reshape(devices, CL_DEV)
    outgoing = (
        placed_rows(queries[0]),
        placed_rows(key_rows[0]),
        placed_rows(value_rows[0]),
        counts,
    )
    arrived = (
        lax.all_to_all(outgoing[0], "ctx", split_axis=0, concat_axis=0, tiled=True),
        lax.all_to_all(outgoing[1], "ctx", split_axis=0, concat_axis=0, tiled=True),
        lax.all_to_all(outgoing[2], "ctx", split_axis=0, concat_axis=0, tiled=True),
        lax.all_to_all(outgoing[3], "ctx", split_axis=0, concat_axis=0, tiled=True),
    )
    attended = attend(arrived[0], arrived[1], arrived[2], arrived[3])
    sums = owner_sums(arrived[0], arrived[1], arrived[3])[None][0]
    back = lax.all_to_all(attended, "ctx", split_axis=0, concat_axis=0, tiled=True)
    mine = back.reshape(clusters * send, width)[where_row]
    projected = jnp.dot(
        lax.all_gather(mine, "head", axis=1, tiled=True),
        out_weight,
        preferred_element_type=jnp.float32,
    ).astype(jnp.bfloat16)
    centroids = sums * lax.rsqrt(jnp.mean(sums * sums, axis=-1, keepdims=True) + norm_eps)
    return (projected, centroids[None])


def solution(mesh):
    in_specs = (
        P("head", "ctx", None),
        P("head", "ctx", None),
        P("head", "ctx", None),
        P("head", "ctx", None),
        P(None, "head"),
    )
    out_specs = (P("ctx", "head"), P("head", "ctx", None))
    return jax.shard_map(shards, mesh=mesh, in_specs=in_specs, out_specs=out_specs, check_vma=False)
```

profile of v0, /device:TPU:0, one launch (start us, length us, event | category | flops | bytes accessed | tf_op | source)
XLA Modules:
  0.0 130.8 jit_solution(9284928553017711196)
XLA Ops:
  0.6 0.0 copy-start
  0.6 0.0 copy-start.4
  0.7 7.9 %scatter_custom_fusion = s32[32]{0:T(128)S(1)} fusion(s32[1024]{0:T(1024)} %bitcast.83, s32[1024]{0:T(1024)S(1)} %broadcast.124, s32[]{:T(128)} %copy.50), kind=kCustom, calls=%fused_computation.64 | custom fusion | flops 1024 | bytes 640 | tf_op jit(solution)/shard_map/scatter-add | solution.py:93
  8.5 0.7 all_to_all.20
  9.2 7.4 %all-to-all-start = ((s32[16,1,2]{2,1,0:T(1,128)}), s32[16,1,2]{2,1,0:T(1,128)S(1)}, u32[]{:S(2)}, u32[]{:S(2)}) async-start(s32[16,1,2]{2,1,0:T(1,128)} %bitcast.5), calls=%async_computation | async-start | bytes 16384 | tf_op jit(solution)/shard_map/all_to_all | solution.py:104
  16.6 9.8 %while.22 = (s32[]{:T(128)}, s32[2,512]{1,0:T(2,128)S(1)}, s32[2]{0:T(128)S(1)}, s32[1024]{0:T(1024)}, s32[1,1024,1]{1,2,0:T(1,128)}, /*index=5*/s32[]{:T(128)}, s32[]{:T(128)}, s32[]{:T(128)}) while((s32[]{:T(128)}, s32[2,512]{1,0:T(2,128)S(1)}, s32[2]{0:T(128)S(1)}, s32[1024]{0:T(1024)}, s32[1,1024,1]{1,2,0:T(1,128)}, ...), condition=%wide.region_2.3_spmd.clone, body=%wide.region_0.2_spmd.clone.sunk | while | flops 2621445 | bytes 20623 | solution.py:27
  16.7 0.6 dynamic_slice.50
  18.9 0.8 dynamic_slice.51
  19.7 0.6 iota_add_fusion.2
  20.3 1.3 convert_reduce_fusion.2
  21.6 0.6 dynamic_slice.50
  23.8 0.8 dynamic_slice.51
  24.6 0.6 iota_add_fusion.2
  25.2 1.3 convert_reduce_fusion.2
  26.5 0.7 compare_select_fusion
  27.2 4.3 %scatter_custom_fusion.2 = bf16[2048,128]{1,0:T(8,128)(2,1)} fusion(s32[1024]{0:T(1024)S(1)} %bitcast.89, bf16[1,1024,128]{2,1,0:T(8,128)(2,1)} %param.10, bf16[]{:T(256)} %constant.17.clone.1), kind=kCustom, calls=%fused_computation.46 | custom fusion | bytes 786434 | tf_op jit(solution)/shard_map/scatter | solution.py:89
  31.5 0.0 all-to-all-done
  31.5 6.0 %all-to-all-start.2 = ((bf16[16,2,64,128]{3,2,1,0:T(8,128)(2,1)}), bf16[16,2,64,128]{3,2,1,0:T(8,128)(2,1)S(1)}, u32[]{:S(2)}, u32[]{:S(2)}) async-start(bf16[16,2,64,128]{3,2,1,0:T(8,128)(2,1)} %bitcast.15), calls=%async_computation.2 | async-start | bytes 1048576 | tf_op jit(solution)/shard_map/all_to_all | solution.py:102
  37.5 4.3 %scatter_custom_fusion.1 = bf16[2048,128]{1,0:T(8,128)(2,1)} fusion(s32[1024]{0:T(1024)S(1)} %bitcast.90, bf16[1,1024,128]{2,1,0:T(8,128)(2,1)} %param.9, bf16[]{:T(256)} %constant.17.clone.1), kind=kCustom, calls=%fused_computation.48 | custom fusion | bytes 786434 | tf_op jit(solution)/shard_map/scatter | solution.py:89
  41.9 9.9 %all-to-all-done.2 = bf16[16,2,64,128]{3,2,1,0:T(8,128)(2,1)S(1)} async-done(((bf16[16,2,64,128]{3,2,1,0:T(8,128)(2,1)}), bf16[16,2,64,128]{3,2,1,0:T(8,128)(2,1)S(1)}, u32[]{:S(2)}, u32[]{:S(2)}) %all-to-all-start.2) | async-done | bytes 524320 | tf_op jit(solution)/shard_map/all_to_all | solution.py:102
  51.8 4.2 %all-to-all-start.1 = ((bf16[16,2,64,128]{3,2,1,0:T(8,128)(2,1)}), bf16[16,2,64,128]{3,2,1,0:T(8,128)(2,1)S(1)}, u32[]{:S(2)}, u32[]{:S(2)}) async-start(bf16[16,2,64,128]{3,2,1,0:T(8,128)(2,1)} %bitcast.11), calls=%async_computation.1 | async-start | bytes 1048576 | tf_op jit(solution)/shard_map/all_to_all | solution.py:101
  56.0 0.0 copy-done.4
  56.0 4.0 %scatter_custom_fusion.3 = bf16[2048,128]{1,0:T(8,128)(2,1)} fusion(s32[1024]{0:T(1024)S(1)} %bitcast.91, bf16[1,1024,128]{2,1,0:T(8,128)(2,1)S(1)} %copy-done.4, bf16[]{:T(256)} %constant.17.clone.1), kind=kCustom, calls=%fused_computation.44 | custom fusion | bytes 786434 | tf_op jit(solution)/shard_map/scatter | solution.py:89
  60.0 0.1 lt.73
  60.1 10.2 %all-to-all-done.1 = bf16[16,2,64,128]{3,2,1,0:T(8,128)(2,1)S(1)} async-done(((bf16[16,2,64,128]{3,2,1,0:T(8,128)(2,1)}), bf16[16,2,64,128]{3,2,1,0:T(8,128)(2,1)S(1)}, u32[]{:S(2)}, u32[]{:S(2)}) %all-to-all-start.1) | async-done | bytes 524320 | tf_op jit(solution)/shard_map/all_to_all | solution.py:101
  70.2 4.2 %all-to-all-start.3 = ((bf16[16,2,64,128]{3,2,1,0:T(8,128)(2,1)}), bf16[16,2,64,128]{3,2,1,0:T(8,128)(2,1)S(1)}, u32[]{:S(2)}, u32[]{:S(2)}) async-start(bf16[16,2,64,128]{3,2,1,0:T(8,128)(2,1)} %bitcast.19), calls=%async_computation.3 | async-start | bytes 1048576 | tf_op jit(solution)/shard_map/all_to_all | solution.py:103
  74.4 0.1 copy.26
  74.5 0.1 copy.31
  74.6 0.1 lt.75
  74.7 0.1 lt.76
  74.8 0.1 iota_compare_fusion.3
  75.0 0.4 fusion.34
  75.4 13.3 %all-to-all-done.3 = bf16[16,2,64,128]{3,2,1,0:T(8,128)(2,1)S(1)} async-done(((bf16[16,2,64,128]{3,2,1,0:T(8,128)(2,1)}), bf16[16,2,64,128]{3,2,1,0:T(8,128)(2,1)S(1)}, u32[]{:S(2)}, u32[]{:S(2)}) %all-to-all-start.3) | async-done | bytes 524320 | tf_op jit(solution)/shard_map/all_to_all | solution.py:103
  88.7 0.8 copy.29
  89.5 6.7 %while.21 = (s32[]{:T(128)}, bf16[2,1024,128]{2,1,0:T(8,128)(2,1)}, s32[2,1024]{1,0:T(2,128)S(1)}, bf16[2,1024,128]{2,1,0:T(8,128)(2,1)S(1)}, bf16[2,1024,128]{2...) while((s32[]{:T(128)}, bf16[2,1024,128]{2,1,0:T(8,128)(2,1)}, s32[2,1024]{1,0:T(2,128)S(1)}, ...), condition=%wide.region_10.11_spmd, body=%wide.region_7.10_spmd.sunk | while | flops 548666368 | bytes 19951780 | solution.py:66
  89.6 0.0 copy-start.1
  89.6 0.0 copy-start.3
  89.6 0.9 fusion.56
  90.5 0.6 fusion.57
  91.1 0.0 copy-done.1
  91.1 0.0 copy-done.3
  91.2 0.9 fusion.58
  92.1 0.0 copy-start.2
  92.1 0.8 copy-done.2
  92.9 0.0 copy-start.1
  92.9 0.0 copy-start.3
  92.9 0.9 fusion.56
  93.8 0.6 fusion.57
  94.5 0.0 copy-done.1
  94.5 0.0 copy-done.3
  94.5 0.9 fusion.58
  95.4 0.0 copy-start.2
  95.4 0.8 copy-done.2
  96.2 1.9 %copy.34 = bf16[2,16,64,128]{3,2,0,1:T(8,128)(2,1)} copy(bf16[2,16,64,128]{3,2,1,0:T(8,128)(2,1)} %bitcast.81) | data formatting | bytes 1048576 | tf_op jit(solution)/shard_map/reshape | solution.py:67
  98.0 4.2 %all-to-all-start.4 = ((bf16[16,2,64,128]{3,2,1,0:T(8,128)(2,1)}), bf16[16,2,64,128]{3,2,1,0:T(8,128)(2,1)S(1)}, u32[]{:S(2)}, u32[]{:S(2)}) async-start(bf16[16,2,64,128]{3,2,1,0:T(8,128)(2,1)} %bitcast.60), calls=%async_computation.4 | async-start | bytes 1048576 | tf_op jit(solution)/shard_map/all_to_all | solution.py:108
  102.2 0.4 fusion.30
  102.6 1.0 fusion.33
  103.6 0.1 multiply_reduce_fusion
  103.7 0.6 bitcast_multiply_fusion
  104.4 12.1 %all-to-all-done.4 = bf16[16,2,64,128]{3,2,1,0:T(8,128)(2,1)S(1)} async-done(((bf16[16,2,64,128]{3,2,1,0:T(8,128)(2,1)}), bf16[16,2,64,128]{3,2,1,0:T(8,128)(2,1)S(1)}, u32[]{:S(2)}, u32[]{:S(2)}) %all-to-all-start.4) | async-done | bytes 524320 | tf_op jit(solution)/shard_map/all_to_all | solution.py:108
  116.5 3.2 %gather_fusion = bf16[1024,128]{1,0:T(8,128)(2,1)S(1)} fusion(bf16[2048,128]{1,0:T(8,128)(2,1)S(1)} %bitcast.75, s32[1024]{0:T(1024)S(1)} %broadcast_clamp_fusion), kind=kCustom, calls=%fused_computation | custom fusion | bytes 528384 | tf_op jit(solution)/shard_map/gather | solution.py:109
  119.7 9.0 %all-gather = bf16[1024,256]{1,0:T(8,128)(2,1)S(1)} all-gather(bf16[1024,128]{1,0:T(8,128)(2,1)S(1)} %gather_fusion), channel_id=2, replica_groups=mesh['ctx'=16,'head'=2] {'head'}, dimensions={1}, use_global_device_ids=true | all-gather | bytes 786432 | tf_op jit(solution)/shard_map/all_gather | solution.py:111
  128.7 0.0 copy-done
  128.7 2.0 %convolution_convert_fusion = bf16[1024,1024]{1,0:T(8,128)(2,1)} fusion(bf16[1024,256]{1,0:T(8,128)(2,1)S(1)} %all-gather, bf16[256,1024]{1,0:T(8,128)(2,1)S(1)} %copy-done), kind=kOutput, calls=%fused_computation.33 | convolution fusion | flops 537919488 | bytes 3145728 | tf_op jit(solution)/shard_map/dot_general | solution.py:110
  (17 shorter events, 0.3 us)
Async XLA Ops:
  0.6 128.1 %copy-start = (bf16[256,1024]{1,0:T(8,128)(2,1)S(1)}, bf16[256,1024]{1,0:T(8,128)(2,1)}, u32[]{:S(2)}) copy-start(bf16[256,1024]{1,0:T(8,128)(2,1)} %param.13) | copy-start | bytes 1572868
  0.6 55.3 %copy-start.4 = (bf16[1,1024,128]{2,1,0:T(8,128)(2,1)S(1)}, bf16[1,1024,128]{2,1,0:T(8,128)(2,1)}, u32[]{:S(2)}) copy-start(bf16[1,1024,128]{2,1,0:T(8,128)(2,1)} %param.11) | copy-start | bytes 786436
  9.2 22.3 %all-to-all-start = ((s32[16,1,2]{2,1,0:T(1,128)}), s32[16,1,2]{2,1,0:T(1,128)S(1)}, u32[]{:S(2)}, u32[]{:S(2)}) async-start(s32[16,1,2]{2,1,0:T(1,128)} %bitcast.5), calls=%async_computation | async-start | bytes 16384 | tf_op jit(solution)/shard_map/all_to_all | solution.py:104
  31.5 20.3 %all-to-all-start.2 = ((bf16[16,2,64,128]{3,2,1,0:T(8,128)(2,1)}), bf16[16,2,64,128]{3,2,1,0:T(8,128)(2,1)S(1)}, u32[]{:S(2)}, u32[]{:S(2)}) async-start(bf16[16,2,64,128]{3,2,1,0:T(8,128)(2,1)} %bitcast.15), calls=%async_computation.2 | async-start | bytes 1048576 | tf_op jit(solution)/shard_map/all_to_all | solution.py:102
  51.8 18.4 %all-to-all-start.1 = ((bf16[16,2,64,128]{3,2,1,0:T(8,128)(2,1)}), bf16[16,2,64,128]{3,2,1,0:T(8,128)(2,1)S(1)}, u32[]{:S(2)}, u32[]{:S(2)}) async-start(bf16[16,2,64,128]{3,2,1,0:T(8,128)(2,1)} %bitcast.11), calls=%async_computation.1 | async-start | bytes 1048576 | tf_op jit(solution)/shard_map/all_to_all | solution.py:101
  70.2 18.4 %all-to-all-start.3 = ((bf16[16,2,64,128]{3,2,1,0:T(8,128)(2,1)}), bf16[16,2,64,128]{3,2,1,0:T(8,128)(2,1)S(1)}, u32[]{:S(2)}, u32[]{:S(2)}) async-start(bf16[16,2,64,128]{3,2,1,0:T(8,128)(2,1)} %bitcast.19), calls=%async_computation.3 | async-start | bytes 1048576 | tf_op jit(solution)/shard_map/all_to_all | solution.py:103
  89.6 1.6 %copy-start.1 = (bf16[2,1024,128]{2,1,0:T(8,128)(2,1)S(1)}, bf16[2,1024,128]{2,1,0:T(8,128)(2,1)}, u32[]{:S(2)}) copy-start(bf16[2,1024,128]{2,1,0:T(8,128)(2,1)} %get-tuple-element.208) | copy-start | bytes 1572868 | tf_op jit(solution)/shard_map/while
  89.6 1.6 %copy-start.3 = (bf16[2,1024,128]{2,1,0:T(8,128)(2,1)S(1)}, bf16[2,1024,128]{2,1,0:T(8,128)(2,1)}, u32[]{:S(2)}) copy-start(bf16[2,1024,128]{2,1,0:T(8,128)(2,1)} %get-tuple-element.219) | copy-start | bytes 1572868 | tf_op jit(solution)/shard_map/while
  92.1 0.8 copy-start.2
  92.9 1.6 %copy-start.1 = (bf16[2,1024,128]{2,1,0:T(8,128)(2,1)S(1)}, bf16[2,1024,128]{2,1,0:T(8,128)(2,1)}, u32[]{:S(2)}) copy-start(bf16[2,1024,128]{2,1,0:T(8,128)(2,1)} %get-tuple-element.208) | copy-start | bytes 1572868 | tf_op jit(solution)/shard_map/while
  92.9 1.6 %copy-start.3 = (bf16[2,1024,128]{2,1,0:T(8,128)(2,1)S(1)}, bf16[2,1024,128]{2,1,0:T(8,128)(2,1)}, u32[]{:S(2)}) copy-start(bf16[2,1024,128]{2,1,0:T(8,128)(2,1)} %get-tuple-element.219) | copy-start | bytes 1572868 | tf_op jit(solution)/shard_map/while
  95.4 0.8 copy-start.2
  98.0 18.4 %all-to-all-start.4 = ((bf16[16,2,64,128]{3,2,1,0:T(8,128)(2,1)}), bf16[16,2,64,128]{3,2,1,0:T(8,128)(2,1)S(1)}, u32[]{:S(2)}, u32[]{:S(2)}) async-start(bf16[16,2,64,128]{3,2,1,0:T(8,128)(2,1)} %bitcast.60), calls=%async_computation.4 | async-start | bytes 1048576 | tf_op jit(solution)/shard_map/all_to_all | solution.py:108
where the time goes:
time: 132 us; the launch traced here: 131 us
  waiting for transfers between devices  45.6 us (35%)
  starting transfers between devices  25.9 us (20%)
  local copies, waits for them, and re-layouts  24.1 us (18%)
  other arithmetic  16.2 us (12%)
  blocking collectives  9.04 us (7%)
  matrix products  5.71 us (4%)
  loops' own time  3.5 us (3%)
    all_to_all x1, waiting for transfers between devices, shards(): lax.all_to_all(outgoing[2], 'ctx', split_axis=0, concat_axis=0, tiled=True)  13.3 us
    scatter x3, local copies, waits for them, and re-layouts, placed_rows(): jnp.zeros((clusters * send, width), values.dtype).at[where_row].set(values)  12.7 us
    all_to_all x1, waiting for transfers between devices, shards(): lax.all_to_all(attended, 'ctx', split_axis=0, concat_axis=0, tiled=True)  12.1 us
    all_to_all x1, waiting for transfers between devices, shards(): lax.all_to_all(outgoing[0], 'ctx', split_axis=0, concat_axis=0, tiled=True)  10.2 us
    all_to_all x1, waiting for transfers between devices, shards(): lax.all_to_all(outgoing[1], 'ctx', split_axis=0, concat_axis=0, tiled=True)  9.94 us
    all_gather x1, blocking collectives, shards(): lax.all_gather(mine, 'head', axis=1, tiled=True)  9.04 us
    scatter-add x1, other arithmetic, shards(): jax.ops.segment_sum(ones, group, num_segments=clusters)  7.88 us
    all_to_all x1, starting transfers between devices, shards(): lax.all_to_all(outgoing[3], 'ctx', split_axis=0, concat_axis=0, tiled=True)  7.39 us
  transfers between devices with their start and end apart: 5, of which 4 were waited for; matrix products, arithmetic and copies ran while one was open for 17% of the time, Pallas kernels for 0%

commit v1 on v0

v1 whole, which is shorter than its diff:
```python
import functools

import jax
import jax.numpy as jnp
from jax import lax
from jax.experimental import pallas as pl
from jax.experimental.pallas import tpu as pltpu
from jax.sharding import PartitionSpec as P

CL_DEV = 2
CAP = 1024
EMPTY = 2.0**100
LOW = -1e30

norm_eps = 1e-06
MESH = pl.DeviceIdType.MESH


def dot_t(a, b):
    return lax.dot_general(a, b, (((1,), (1,)), ((), ())), preferred_element_type=jnp.float32)


def unit_rows(values):
    return values * lax.rsqrt(jnp.mean(values * values, axis=-1, keepdims=True) + norm_eps)


def slots_of(ids, clusters, send):
    tokens = ids.shape[1]
    step = min(256, tokens)
    names = lax.broadcasted_iota(jnp.int32, (clusters, step), 0)
    before = lax.broadcasted_iota(jnp.int32, (step, step), 0)
    after = lax.broadcasted_iota(jnp.int32, (step, step), 1)
    earlier = jnp.where(before < after, 1.0, 0.0).astype(jnp.bfloat16)
    carry = jnp.zeros((clusters, 1), jnp.float32)
    out = []
    for start in range(0, tokens, step):
        part = ids[:, start : start + step]
        named = jnp.where(names == part, 1.0, 0.0)
        count = jnp.dot(named.astype(jnp.bfloat16), earlier, preferred_element_type=jnp.float32)
        rank = jnp.sum(named * (count + carry), axis=0, keepdims=True)
        carry = carry + jnp.sum(named, axis=1, keepdims=True)
        out.append(part * send + rank.astype(jnp.int32))
    return jnp.concatenate(out, axis=1)


def kernel(n, heads, send, q_hbm, k_hbm, v_hbm, ids_ref, joined_ref, cent_ref,
           rows, msg, recv, att, back, keys, bias, in_sem, f_send, f_recv, b_send, b_recv, h_send, h_recv):
    tokens, width = q_hbm.shape[1], q_hbm.shape[2]
    pack = CL_DEV * send
    clusters = CL_DEV * n
    me = lax.axis_index("ctx")
    head = lax.axis_index("head")

    loads = []
    for i, ref in enumerate((q_hbm, k_hbm, v_hbm)):
        load = pltpu.make_async_copy(ref.at[0], rows.at[:, i * width : (i + 1) * width], in_sem.at[i])
        load.start()
        loads.append(load)

    barrier = pltpu.get_barrier_semaphore()

    def greet(i, carry):
        pl.semaphore_signal(barrier, inc=1, device_id=(lax.rem(me + i, n), head), device_id_type=MESH)
        return carry

    lax.fori_loop(1, n, greet, 0)
    for i in range(1, heads):
        pl.semaphore_signal(barrier, inc=1, device_id=(me, lax.rem(head + i, heads)), device_id_type=MESH)

    slot_row = slots_of(ids_ref[...], clusters, send)
    slot_col = jnp.transpose(jnp.broadcast_to(slot_row, (128, tokens)))
    rows[:, 3 * width :] = jnp.ones((tokens, width), jnp.bfloat16)
    for load in loads:
        load.wait()

    chunk = max(128, pack)
    peers = chunk // pack
    chunks = n // peers
    chunk_iota = lax.broadcasted_iota(jnp.int32, (chunk, tokens), 0)
    mine = me // peers

    def fill(c):
        place = jnp.where(chunk_iota + c * chunk == slot_row, 1.0, 0.0).astype(jnp.bfloat16)
        placed = jnp.dot(place, rows[...], preferred_element_type=jnp.float32)
        held = placed[:, 3 * width :]
        part = jnp.concatenate(
            [
                placed[:, :width],
                jnp.where(held > 0.5, placed[:, width : 2 * width], EMPTY),
                placed[:, 2 * width : 3 * width],
            ],
            axis=1,
        ).astype(jnp.bfloat16)
        msg[pl.ds(c * peers, peers)] = part.reshape(peers, pack, 3 * width)

    def forward(d):
        return pltpu.make_async_remote_copy(
            src_ref=msg.at[d], dst_ref=recv.at[me], send_sem=f_send.at[d], recv_sem=f_recv.at[me],
            device_id=(d, head), device_id_type=MESH)

    def ship(c):
        for i in range(peers):
            d = c * peers + i

            @pl.when(d != me)
            def _():
                forward(d).start()

    half = chunks // 2
    order = lambda i: lax.rem(mine + half + i, chunks)
    fill(order(0))
    pl.semaphore_wait(barrier, n - 1 + heads - 1)

    def dispatch(i, carry):
        fill(order(i))
        ship(order(i - 1))
        return carry

    lax.fori_loop(1, chunks, dispatch, 0)
    ship(order(chunks - 1))
    recv[me] = msg[me]

    def arrived(s):
        @pl.when(s != me)
        def _():
            pltpu.make_async_remote_copy(
                src_ref=msg.at[s], dst_ref=recv.at[s], send_sem=f_send.at[s], recv_sem=f_recv.at[s],
                device_id=(me, head), device_id_type=MESH).wait_recv()

    def returned(s):
        return pltpu.make_async_remote_copy(
            src_ref=att.at[s], dst_ref=back.at[me], send_sem=b_send.at[s], recv_sem=b_recv.at[me],
            device_id=(s, head), device_id_type=MESH)

    block = 256
    sources = block // send
    tri_r = lax.broadcasted_iota(jnp.int32, (block, block), 0)
    tri_c = lax.broadcasted_iota(jnp.int32, (block, block), 1)
    causal = jnp.where(tri_c <= tri_r, 0.0, LOW)
    ones = jnp.ones((8, width), jnp.bfloat16)
    sums = [jnp.zeros((1, width), jnp.float32) for _ in range(CL_DEV)]
    scale = jnp.float32(width ** (-0.5))

    for b in range(CAP // block):
        first, last = b * sources, (b + 1) * sources

        def wait_one(s, carry):
            arrived(s)
            return carry

        lax.fori_loop(first, last, wait_one, 0)
        span = (b + 1) * block
        for j in range(CL_DEV):
            inner = slice(j * send, (j + 1) * send)
            q = recv[first:last, inner, :width].reshape(block, width)
            k32 = recv[first:last, inner, width : 2 * width].reshape(block, width).astype(jnp.float32)
            vacant = k32 > 0.5 * EMPTY
            k32 = jnp.where(vacant, 0.0, k32)
            keys[j, b * block : span, :] = k32.astype(jnp.bfloat16)
            flags = dot_t(ones, jnp.where(vacant, 1.0, 0.0).astype(jnp.bfloat16))
            bias[j, :, b * block : span] = jnp.where(flags > 0.5, LOW, 0.0)
            unit = unit_rows(q.astype(jnp.float32)) + unit_rows(k32)
            sums[j] = sums[j] + jnp.sum(unit, axis=0, keepdims=True)
            scores = dot_t(q, keys[j, :span, :]) * scale + bias[j, 0:1, :span]
            tail = scores[:, b * block :] + causal
            scores = tail if b == 0 else jnp.concatenate([scores[:, : b * block], tail], axis=1)
            highest = jnp.max(scores, axis=1, keepdims=True)
            weights = jnp.exp(scores - highest)
            total = jnp.sum(weights, axis=1, keepdims=True)
            v = recv[:last, inner, 2 * width :].reshape(span, width)
            mixed = jnp.dot(weights.astype(jnp.bfloat16), v, preferred_element_type=jnp.float32)
            att[first:last, inner, :] = (mixed / total).astype(jnp.bfloat16).reshape(sources, send, width)

        def give_one(s, carry):
            @pl.when(s != me)
            def _():
                returned(s).start()

            return carry

        lax.fori_loop(first, last, give_one, 0)

    for j in range(CL_DEV):
        mean = jnp.mean(sums[j] * sums[j], axis=-1, keepdims=True)
        cent_ref[j : j + 1, :] = sums[j] * lax.rsqrt(mean + norm_eps)
    back[me] = att[me]

    slots = CL_DEV * CAP
    step = 256
    group = step // pack
    lanes = lax.broadcasted_iota(jnp.int32, (tokens, 128), 1)
    got = jnp.zeros((tokens, width), jnp.float32)
    for c in range(slots // step):

        def wait_back(s, carry):
            @pl.when(s != me)
            def _():
                pltpu.make_async_remote_copy(
                    src_ref=att.at[s], dst_ref=back.at[s], send_sem=b_send.at[s], recv_sem=b_recv.at[s],
                    device_id=(me, head), device_id_type=MESH).wait_recv()

            return carry

        lax.fori_loop(c * group, (c + 1) * group, wait_back, 0)
        pick = jnp.concatenate(
            [jnp.where(slot_col == lanes + (c * step + i), 1.0, 0.0) for i in range(0, step, 128)], axis=1
        ).astype(jnp.bfloat16)
        piece = back[c * group : (c + 1) * group].reshape(step, width)
        got = got + jnp.dot(pick, piece, preferred_element_type=jnp.float32)

    own = pl.ds(pl.multiple_of(head * width, width), width)
    joined_ref[:, own] = got.astype(jnp.bfloat16)

    def share(i):
        return pltpu.make_async_remote_copy(
            src_ref=joined_ref.at[:, own], dst_ref=joined_ref.at[:, own],
            send_sem=h_send.at[i - 1], recv_sem=h_recv.at[i - 1],
            device_id=(me, lax.rem(head + i, heads)), device_id_type=MESH)

    for i in range(1, heads):
        share(i).start()

    def sent(i, carry):
        d = lax.rem(me + i, n)
        forward(d).wait_send()
        returned(d).wait_send()
        return carry

    lax.fori_loop(1, n, sent, 0)
    for i in range(1, heads):
        share(i).wait_send()
        other = pl.ds(pl.multiple_of(lax.rem(head + heads - i, heads) * width, width), width)
        pltpu.make_async_remote_copy(
            src_ref=joined_ref.at[:, other], dst_ref=joined_ref.at[:, other],
            send_sem=h_send.at[i - 1], recv_sem=h_recv.at[i - 1],
            device_id=(me, head), device_id_type=MESH).wait_recv()


def shards(n, heads, queries, key_rows, value_rows, cluster_ids, out_weight):
    tokens, width = queries.shape[1], queries.shape[2]
    send = CAP // n
    pack = CL_DEV * send
    bf16, f32 = jnp.bfloat16, jnp.float32
    dma = pltpu.SemaphoreType.DMA
    joined, centroids = pl.pallas_call(
        functools.partial(kernel, n, heads, send),
        out_shape=(
            jax.ShapeDtypeStruct((tokens, heads * width), bf16),
            jax.ShapeDtypeStruct((CL_DEV, width), f32),
        ),
        in_specs=[pl.BlockSpec(memory_space=pl.ANY)] * 3 + [pl.BlockSpec(memory_space=pltpu.VMEM)],
        out_specs=(pl.BlockSpec(memory_space=pltpu.VMEM), pl.BlockSpec(memory_space=pltpu.VMEM)),
        scratch_shapes=[
            pltpu.VMEM((tokens, 4 * width), bf16),
            pltpu.VMEM((n, pack, 3 * width), bf16),
            pltpu.VMEM((n, pack, 3 * width), bf16),
            pltpu.VMEM((n, pack, width), bf16),
            pltpu.VMEM((n, pack, width), bf16),
            pltpu.VMEM((CL_DEV, CAP, width), bf16),
            pltpu.VMEM((CL_DEV, 8, CAP), f32),
            dma((3,)),
            dma((n,)),
            dma((n,)),
            dma((n,)),
            dma((n,)),
            dma((max(1, heads - 1),)),
            dma((max(1, heads - 1),)),
        ],
        compiler_params=pltpu.CompilerParams(
            collective_id=0, has_side_effects=True, vmem_limit_bytes=48 * 1024 * 1024
        ),
        name="route",
    )(queries, key_rows, value_rows, cluster_ids[0, :, 0][None, :])
    projected = jnp.dot(joined, out_weight, preferred_element_type=f32).astype(bf16)
    return (projected, centroids[None])


def solution(mesh):
    in_specs = (
        P("head", "ctx", None),
        P("head", "ctx", None),
        P("head", "ctx", None),
        P("head", "ctx", None),
        P(None, "head"),
    )
    out_specs = (P("ctx", "head"), P("head", "ctx", None))
    body = functools.partial(shards, mesh.shape["ctx"], mesh.shape["head"])
    return jax.shard_map(body, mesh=mesh, in_specs=in_specs, out_specs=out_specs, check_vma=False)
```

time: 132 us -> 69.7 us (0.53)
  the two profiles are of different devices: /device:TPU:0 before, /device:TPU:26 now
where the time goes in v1:
time: 69.7 us; the launch traced here: 69.5 us
  Pallas kernels  62.6 us (90%)
  local copies, waits for them, and re-layouts  4.16 us (6%)
  matrix products  2.04 us (3%)
    pallas_call x1, Pallas kernels, shards(): pl.pallas_call(functools.partial(kernel, n, heads, send), out_shape=(jax....  62.6 us
    unnamed x11, local copies, waits for them, and re-layouts  4.16 us
    dot_general x1, matrix products, shards(): jnp.dot(joined, out_weight, preferred_element_type=f32).astype(bf16)  2.04 us

profile of v1, /device:TPU:26, one launch (start us, length us, event | category | flops | bytes accessed | tf_op | source)
XLA Modules:
  0.0 69.5 jit_solution(1082743818373680236)
XLA Ops:
  0.6 0.0 copy-start
  0.6 0.0 copy-start.1
  0.7 1.0 %copy-done.1 = bf16[1,1024,128]{2,1,0:T(8,128)(2,1)S(1)} copy-done((bf16[1,1024,128]{2,1,0:T(8,128)(2,1)S(1)}, bf16[1,1024,128]{2,1,0:T(8,128)(2,1)}, u32[]{:S(2)}) %copy-start.1) | copy-done | bytes 262168
  1.7 0.0 copy-start.2
  1.7 0.9 %copy-done.2 = bf16[1,1024,128]{2,1,0:T(8,128)(2,1)S(1)} copy-done((bf16[1,1024,128]{2,1,0:T(8,128)(2,1)S(1)}, bf16[1,1024,128]{2,1,0:T(8,128)(2,1)}, u32[]{:S(2)}) %copy-start.2) | copy-done | bytes 262168
  2.6 0.0 copy-start.3
  2.6 0.9 %copy-done.3 = bf16[1,1024,128]{2,1,0:T(8,128)(2,1)S(1)} copy-done((bf16[1,1024,128]{2,1,0:T(8,128)(2,1)S(1)}, bf16[1,1024,128]{2,1,0:T(8,128)(2,1)}, u32[]{:S(2)}) %copy-start.3) | copy-done | bytes 262168
  3.6 0.0 copy-start.4
  3.6 0.7 copy-done.4
  4.2 62.6 %route.1 = (bf16[1024,256]{1,0:T(8,128)(2,1)S(1)}, f32[2,128]{1,0:T(2,128)S(1)}) custom-call(bf16[1,1024,128]{2,1,0:T(8,128)(2,1)S(1)} %copy-done.1, bf16[1,1024,128]{2,1,0:T(8,128)(2,1)S(1)} %copy-done.2, bf16[1,1024,128]{2,1,0:T(8,128)(2,1)S(1)} %copy-done.3, s32[1,1024]{1,0:T(1,128)S(1)} %bitcast.4), custom_call_target="tpu_custom_call" | custom-call | tf_op jit(solution)/shard_map/route/pallas_call | solution.py:245
  66.9 0.0 copy-done
  66.9 2.0 %convolution_convert_fusion = bf16[1024,1024]{1,0:T(8,128)(2,1)} fusion(bf16[1024,256]{1,0:T(8,128)(2,1)S(1)} %get-tuple-element.4, bf16[256,1024]{1,0:T(8,128)(2,1)S(1)} %copy-done), kind=kOutput, calls=%fused_computation | convolution fusion | flops 537919488 | bytes 3145728 | tf_op jit(solution)/shard_map/dot_general | solution.py:274
  68.9 0.6 copy.8
Async XLA Ops:
  0.6 66.2 %copy-start = (bf16[256,1024]{1,0:T(8,128)(2,1)S(1)}, bf16[256,1024]{1,0:T(8,128)(2,1)}, u32[]{:S(2)}) copy-start(bf16[256,1024]{1,0:T(8,128)(2,1)} %param.9) | copy-start | bytes 1572868
  0.6 1.0 %copy-start.1 = (bf16[1,1024,128]{2,1,0:T(8,128)(2,1)S(1)}, bf16[1,1024,128]{2,1,0:T(8,128)(2,1)}, u32[]{:S(2)}) copy-start(bf16[1,1024,128]{2,1,0:T(8,128)(2,1)} %q_hbm.1) | copy-start | bytes 786436
  1.7 0.9 %copy-start.2 = (bf16[1,1024,128]{2,1,0:T(8,128)(2,1)S(1)}, bf16[1,1024,128]{2,1,0:T(8,128)(2,1)}, u32[]{:S(2)}) copy-start(bf16[1,1024,128]{2,1,0:T(8,128)(2,1)} %k_hbm.1) | copy-start | bytes 786436
  2.6 0.9 %copy-start.3 = (bf16[1,1024,128]{2,1,0:T(8,128)(2,1)S(1)}, bf16[1,1024,128]{2,1,0:T(8,128)(2,1)}, u32[]{:S(2)}) copy-start(bf16[1,1024,128]{2,1,0:T(8,128)(2,1)} %v_hbm.1) | copy-start | bytes 786436
  3.6 0.7 copy-start.4

commit v2 on v1

v2 whole, which is shorter than its diff:
```python
import functools

import jax
import jax.numpy as jnp
from jax import lax
from jax.experimental import pallas as pl
from jax.experimental.pallas import tpu as pltpu
from jax.sharding import PartitionSpec as P

CL_DEV = 2
CAP = 1024
QUARTERS = 4
EMPTY = 2.0**100
LOW = -1e30

norm_eps = 1e-06
MESH = pl.DeviceIdType.MESH


def dot_t(a, b):
    return lax.dot_general(a, b, (((1,), (1,)), ((), ())), preferred_element_type=jnp.float32)


def unit_rows(values):
    return values * lax.rsqrt(jnp.mean(values * values, axis=-1, keepdims=True) + norm_eps)


def slots_of(ids, clusters, send):
    tokens = ids.shape[1]
    step = min(256, tokens)
    names = lax.broadcasted_iota(jnp.int32, (clusters, step), 0)
    before = lax.broadcasted_iota(jnp.int32, (step, step), 0)
    after = lax.broadcasted_iota(jnp.int32, (step, step), 1)
    earlier = jnp.where(before < after, 1.0, 0.0).astype(jnp.bfloat16)
    carry = jnp.zeros((clusters, 1), jnp.float32)
    out = []
    for start in range(0, tokens, step):
        part = ids[:, start : start + step]
        named = jnp.where(names == part, 1.0, 0.0)
        count = jnp.dot(named.astype(jnp.bfloat16), earlier, preferred_element_type=jnp.float32)
        rank = jnp.sum(named * (count + carry), axis=0, keepdims=True)
        carry = carry + jnp.sum(named, axis=1, keepdims=True)
        out.append(part * send + rank.astype(jnp.int32))
    return jnp.concatenate(out, axis=1)


def kernel(n, heads, send, q_hbm, k_hbm, v_hbm, ids_ref, joined_ref, cent_ref,
           rows, msg, recv, att, back, keys, bias, sums, gathered,
           in_sem, f_send, f_recv, b_send, b_recv, c_send, c_recv, h_send, h_recv):
    tokens, width = q_hbm.shape[1], q_hbm.shape[2]
    clusters = CL_DEV * n
    part = n // QUARTERS
    owned = clusters // (2 * part)
    pack = owned * send
    me = lax.axis_index("ctx")
    head = lax.axis_index("head")
    zone = me // part
    spot = lax.rem(me, part)

    loads = []
    for i, ref in enumerate((q_hbm, k_hbm, v_hbm)):
        load = pltpu.make_async_copy(ref.at[0], rows.at[:, i * width : (i + 1) * width], in_sem.at[i])
        load.start()
        loads.append(load)

    barrier = pltpu.get_barrier_semaphore()

    def greet(i, carry):
        pl.semaphore_signal(barrier, inc=1, device_id=(lax.rem(me + i, n), head), device_id_type=MESH)
        return carry

    lax.fori_loop(1, n, greet, 0)
    for i in range(1, heads):
        pl.semaphore_signal(barrier, inc=1, device_id=(me, lax.rem(head + i, heads)), device_id_type=MESH)

    slot_row = slots_of(ids_ref[...], clusters, send)
    slot_col = jnp.transpose(jnp.broadcast_to(slot_row, (128, tokens)))
    rows[:, 3 * width :] = jnp.ones((tokens, width), jnp.bfloat16)
    for load in loads:
        load.wait()

    chunk = 256
    peers = chunk // pack
    chunks = part // peers
    chunk_iota = lax.broadcasted_iota(jnp.int32, (chunk, tokens), 0)

    def fill(kind, c):
        base = (kind * chunks + c) * chunk
        place = jnp.where(chunk_iota + base == slot_row, 1.0, 0.0).astype(jnp.bfloat16)
        placed = jnp.dot(place, rows[...], preferred_element_type=jnp.float32)
        held = placed[:, 3 * width :]
        new = jnp.concatenate(
            [
                placed[:, :width],
                jnp.where(held > 0.5, placed[:, width : 2 * width], EMPTY),
                placed[:, 2 * width : 3 * width],
            ],
            axis=1,
        ).astype(jnp.bfloat16)
        msg[kind, pl.ds(c * peers, peers)] = new.reshape(peers, pack, 3 * width)

    def forward(kind, spot_to, zone_to, source, whole):
        cols = slice(0, 3 * width) if whole else slice(width, 3 * width)
        d = zone_to * part + spot_to
        return pltpu.make_async_remote_copy(
            src_ref=msg.at[kind, spot_to, :, cols], dst_ref=recv.at[kind, source, :, cols],
            send_sem=f_send.at[kind, d], recv_sem=f_recv.at[kind, source],
            device_id=(d, head), device_id_type=MESH)

    def each_send(kind, i, act, local):
        @pl.when(kind == 1)
        def _():
            @pl.when(zone < 2)
            def _():
                act(forward(1, i, 2, me, False))

            @pl.when(zone == 0)
            def _():
                act(forward(1, i, 1, me, False))

            @pl.when(zone == 3)
            def _():
                act(forward(1, i, 2, me, True))

        @pl.when(kind == 0)
        def _():
            @pl.when(zone == 0)
            def _():
                act(forward(0, i, 1, me, False))

            @pl.when(zone >= 2)
            def _():
                act(forward(0, i, 1, me, True))

        @pl.when((zone < 3 - (1 - kind)) & (i != spot))
        def _():
            act(forward(kind, i, zone, me, True))

        if local:
            @pl.when((zone < 3 - (1 - kind)) & (i == spot))
            def _():
                recv[kind, me] = msg[kind, i]

    def ship(t):
        kind, c = kind_of(t), lax.rem(t, chunks)
        for p in range(peers):
            each_send(kind, c * peers + p, lambda copy: copy.start(), True)

    def kind_of(t):
        return lax.rem(1 - zone // 2 + t // chunks, 2)

    fill(kind_of(0), 0)
    pl.semaphore_wait(barrier, n - 1 + heads - 1)

    def dispatch(t, carry):
        fill(kind_of(t), lax.rem(t, chunks))
        ship(t - 1)
        return carry

    lax.fori_loop(1, 2 * chunks, dispatch, 0)
    ship(2 * chunks - 1)

    unit = unit_rows(rows[:, :width].astype(jnp.float32)) + unit_rows(rows[:, width : 2 * width].astype(jnp.float32))
    upper = unit.astype(jnp.bfloat16)
    lower = (unit - upper.astype(jnp.float32)).astype(jnp.bfloat16)
    names = lax.broadcasted_iota(jnp.int32, (clusters, tokens), 0)
    named = jnp.where(names == ids_ref[...], 1.0, 0.0).astype(jnp.bfloat16)
    local_sums = jnp.dot(named, upper, preferred_element_type=jnp.float32) + jnp.dot(
        named, lower, preferred_element_type=jnp.float32)
    sums[...] = local_sums.reshape(n, CL_DEV, width)

    def summed(d, source):
        return pltpu.make_async_remote_copy(
            src_ref=sums.at[d], dst_ref=gathered.at[source], send_sem=c_send.at[d], recv_sem=c_recv.at[source],
            device_id=(d, head), device_id_type=MESH)

    def send_sums(i, carry):
        summed(lax.rem(me + i, n), me).start()
        return carry

    gathered[me] = sums[me]
    lax.fori_loop(1, n, send_sums, 0)

    def arrived(kind, first, whole):
        def one(s, carry):
            @pl.when(s != me)
            def _():
                cols = slice(0, 3 * width) if whole else slice(width, 3 * width)
                pltpu.make_async_remote_copy(
                    src_ref=msg.at[kind, 0, :, cols], dst_ref=recv.at[kind, s, :, cols],
                    send_sem=f_send.at[kind, s], recv_sem=f_recv.at[kind, s],
                    device_id=(me, head), device_id_type=MESH).wait_recv()

            return carry

        lax.fori_loop(first * part, (first + 1) * part, one, 0)

    def returned(kind, d):
        return pltpu.make_async_remote_copy(
            src_ref=att.at[kind, d], dst_ref=back.at[kind, spot], send_sem=b_send.at[kind, d],
            recv_sem=b_recv.at[kind, spot], device_id=(d, head), device_id_type=MESH)

    block = part * send
    tri_r = lax.broadcasted_iota(jnp.int32, (block, block), 0)
    tri_c = lax.broadcasted_iota(jnp.int32, (block, block), 1)
    causal = jnp.where(tri_c <= tri_r, 0.0, LOW)
    ones = jnp.ones((8, width), jnp.bfloat16)
    scale = jnp.float32(width ** (-0.5))

    def prepare(kind, p, j):
        inner = pl.ds(pl.multiple_of(j * send, send), send)
        lanes = slice(p * block, (p + 1) * block)
        k32 = recv[kind, p * part : (p + 1) * part, inner, width : 2 * width].reshape(block, width).astype(jnp.float32)
        vacant = k32 > 0.5 * EMPTY
        keys[kind, j, lanes, :] = jnp.where(vacant, 0.0, k32).astype(jnp.bfloat16)
        flags = dot_t(ones, jnp.where(vacant, 1.0, 0.0).astype(jnp.bfloat16))
        bias[kind, j, :, lanes] = jnp.where(flags > 0.5, LOW, 0.0)

    def attend(kind, p, j):
        inner = pl.ds(pl.multiple_of(j * send, send), send)
        first, last, span = p * part, (p + 1) * part, (p + 1) * block
        q = recv[kind, first:last, inner, :width].reshape(block, width)
        scores = dot_t(q, keys[kind, j, :span, :]) * scale + bias[kind, j, 0:1, :span]
        tail = scores[:, p * block :] + causal
        scores = tail if p == 0 else jnp.concatenate([scores[:, : p * block], tail], axis=1)
        highest = jnp.max(scores, axis=1, keepdims=True)
        weights = jnp.exp(scores - highest)
        total = jnp.sum(weights, axis=1, keepdims=True)
        v = recv[kind, :last, inner, 2 * width :].reshape(span, width)
        mixed = jnp.dot(weights.astype(jnp.bfloat16), v, preferred_element_type=jnp.float32)
        att[kind, first:last, inner, :] = (mixed / total).astype(jnp.bfloat16).reshape(part, send, width)

    def paired(act):
        def two(jj, carry):
            act(2 * jj)
            act(2 * jj + 1)
            return carry

        lax.fori_loop(0, owned // 2, two, 0)

    def ready(kind, p, whole):
        arrived(kind, p, whole)
        paired(lambda j: prepare(kind, p, j))

    def answer(kind, p):
        paired(lambda j: attend(kind, p, j))

        def one(s, carry):
            @pl.when(s != me)
            def _():
                returned(kind, s).start()

            @pl.when(s == me)
            def _():
                back[kind, spot] = att[kind, s]

            return carry

        lax.fori_loop(p * part, (p + 1) * part, one, 0)

    @pl.when(zone == 0)
    def _():
        for kind in (1, 0):
            ready(kind, 0, True)
            answer(kind, 0)

    @pl.when(zone == 1)
    def _():
        for kind in (1, 0):
            ready(kind, 0, False)
            ready(kind, 1, True)
            answer(kind, 1)
        for p in (2, 3):
            ready(0, p, True)
            answer(0, p)

    @pl.when(zone == 2)
    def _():
        ready(1, 0, False)
        ready(1, 1, False)
        for p in (2, 3):
            ready(1, p, True)
            answer(1, p)

    slots = clusters * send
    lanes = lax.broadcasted_iota(jnp.int32, (tokens, 128), 1)
    got = jnp.zeros((tokens, width), jnp.float32)
    for c in range(slots // chunk):
        kind, start = c // chunks, (c % chunks) * peers
        giver = jnp.minimum(zone, kind + 1) * part

        def wait_back(s, carry):
            @pl.when(giver + s != me)
            def _():
                pltpu.make_async_remote_copy(
                    src_ref=att.at[kind, s], dst_ref=back.at[kind, s], send_sem=b_send.at[kind, s],
                    recv_sem=b_recv.at[kind, s], device_id=(me, head), device_id_type=MESH).wait_recv()

            return carry

        lax.fori_loop(start, start + peers, wait_back, 0)
        pick = jnp.concatenate(
            [jnp.where(slot_col == lanes + (c * chunk + i), 1.0, 0.0) for i in range(0, chunk, 128)], axis=1
        ).astype(jnp.bfloat16)
        piece = back[kind, start : start + peers].reshape(chunk, width)
        got = got + jnp.dot(pick, piece, preferred_element_type=jnp.float32)

    own = pl.ds(pl.multiple_of(head * width, width), width)
    joined_ref[:, own] = got.astype(jnp.bfloat16)

    def share(i):
        return pltpu.make_async_remote_copy(
            src_ref=joined_ref.at[:, own], dst_ref=joined_ref.at[:, own],
            send_sem=h_send.at[i - 1], recv_sem=h_recv.at[i - 1],
            device_id=(me, lax.rem(head + i, heads)), device_id_type=MESH)

    for i in range(1, heads):
        share(i).start()

    def finish(i, carry):
        s = lax.rem(me + i, n)
        summed(s, s).wait_recv()
        summed(s, me).wait_send()
        return carry

    lax.fori_loop(1, n, finish, 0)
    totals = jnp.sum(gathered[...], axis=0)
    mean = jnp.mean(totals * totals, axis=-1, keepdims=True)
    cent_ref[...] = totals * lax.rsqrt(mean + norm_eps)

    def settle(i, carry):
        each_send(0, i, lambda copy: copy.wait_send(), False)
        each_send(1, i, lambda copy: copy.wait_send(), False)
        return carry

    lax.fori_loop(0, part, settle, 0)

    def given(kind, p):
        def one(s, carry):
            @pl.when(s != me)
            def _():
                returned(kind, s).wait_send()

            return carry

        lax.fori_loop(p * part, (p + 1) * part, one, 0)

    @pl.when(zone == 0)
    def _():
        given(1, 0)
        given(0, 0)

    @pl.when(zone == 1)
    def _():
        given(1, 1)
        for p in (1, 2, 3):
            given(0, p)

    @pl.when(zone == 2)
    def _():
        for p in (2, 3):
            given(1, p)

    for i in range(1, heads):
        share(i).wait_send()
        other = pl.ds(pl.multiple_of(lax.rem(head + heads - i, heads) * width, width), width)
        pltpu.make_async_remote_copy(
            src_ref=joined_ref.at[:, other], dst_ref=joined_ref.at[:, other],
            send_sem=h_send.at[i - 1], recv_sem=h_recv.at[i - 1],
            device_id=(me, head), device_id_type=MESH).wait_recv()


def shards(n, heads, queries, key_rows, value_rows, cluster_ids, out_weight):
    tokens, width = queries.shape[1], queries.shape[2]
    send = CAP // n
    part = n // QUARTERS
    owned = CL_DEV * n // (2 * part)
    pack = owned * send
    bf16, f32 = jnp.bfloat16, jnp.float32
    dma = pltpu.SemaphoreType.DMA
    joined, centroids = pl.pallas_call(
        functools.partial(kernel, n, heads, send),
        out_shape=(
            jax.ShapeDtypeStruct((tokens, heads * width), bf16),
            jax.ShapeDtypeStruct((CL_DEV, width), f32),
        ),
        in_specs=[pl.BlockSpec(memory_space=pl.ANY)] * 3 + [pl.BlockSpec(memory_space=pltpu.VMEM)],
        out_specs=(pl.BlockSpec(memory_space=pltpu.VMEM), pl.BlockSpec(memory_space=pltpu.VMEM)),
        scratch_shapes=[
            pltpu.VMEM((tokens, 4 * width), bf16),
            pltpu.VMEM((2, part, pack, 3 * width), bf16),
            pltpu.VMEM((2, n, pack, 3 * width), bf16),
            pltpu.VMEM((2, n, pack, width), bf16),
            pltpu.VMEM((2, part, pack, width), bf16),
            pltpu.VMEM((2, owned, CAP, width), bf16),
            pltpu.VMEM((2, owned, 8, CAP), f32),
            pltpu.VMEM((n, CL_DEV, width), f32),
            pltpu.VMEM((n, CL_DEV, width), f32),
            dma((3,)),
            dma((2, n)),
            dma((2, n)),
            dma((2, n)),
            dma((2, part)),
            dma((n,)),
            dma((n,)),
            dma((max(1, heads - 1),)),
            dma((max(1, heads - 1),)),
        ],
        compiler_params=pltpu.CompilerParams(
            collective_id=0, has_side_effects=True, vmem_limit_bytes=60 * 1024 * 1024
        ),
        name="route",
    )(queries, key_rows, value_rows, cluster_ids[0, :, 0][None, :])
    projected = jnp.dot(joined, out_weight, preferred_element_type=f32).astype(bf16)
    return (projected, centroids[None])


def solution(mesh):
    in_specs = (
        P("head", "ctx", None),
        P("head", "ctx", None),
        P("head", "ctx", None),
        P("head", "ctx", None),
        P(None, "head"),
    )
    out_specs = (P("ctx", "head"), P("head", "ctx", None))
    body = functools.partial(shards, mesh.shape["ctx"], mesh.shape["head"])
    return jax.shard_map(body, mesh=mesh, in_specs=in_specs, out_specs=out_specs, check_vma=False)
```

time: 69.7 us -> 82.3 us (1.18)
  Pallas kernels: 62.6 us -> 77.7 us
  local copies, waits for them, and re-layouts: 4.16 us -> 0.58 us
  matrix products: 2.04 us -> 3.07 us
    pallas_call x1, Pallas kernels: 62.6 us -> 77.7 us  [shards(): pl.pallas_call(functools.partial(kernel, n, heads, send), out_shape=(jax....]
    unnamed x11 -> x5, local copies, waits for them, and re-layouts: 4.16 us -> 0.58 us
    dot_general x1, matrix products: 2.04 us -> 3.07 us  [shards(): jnp.dot(joined, out_weight, preferred_element_type=f32).astype(bf16)]
where the time goes in v2:
time: 82.3 us; the launch traced here: 82 us
  Pallas kernels  77.7 us (94%)
  matrix products  3.07 us (4%)
    pallas_call x1, Pallas kernels, shards(): pl.pallas_call(functools.partial(kernel, n, heads, send), out_shape=(jax....  77.7 us
    dot_general x1, matrix products, shards(): jnp.dot(joined, out_weight, preferred_element_type=f32).astype(bf16)  3.07 us

profile of v2, /device:TPU:26, one launch (start us, length us, event | category | flops | bytes accessed | tf_op | source)
XLA Modules:
  0.0 82.0 jit_solution(5622412442324840357)
XLA Ops:
  0.6 0.0 copy-start
  0.6 77.7 %route.1 = (bf16[1024,256]{1,0:T(8,128)(2,1)}, f32[2,128]{1,0:T(2,128)}) custom-call(bf16[1,1024,128]{2,1,0:T(8,128)(2,1)} %q_hbm.1, bf16[1,1024,128]{2,1,0:T(8,128)(2,1)} %k_hbm.1, bf16[1,1024,128]{2,1,0:T(8,128)(2,1)} %v_hbm.1, s32[1,1024]{1,0:T(1,128)} %bitcast.4), custom_call_target="tpu_custom_call" | custom-call | tf_op jit(solution)/shard_map/route/pallas_call | solution.py:381
  78.4 0.0 copy-start.1
  78.4 0.0 copy-done
  78.4 3.1 %convolution_convert_fusion = bf16[1024,1024]{1,0:T(8,128)(2,1)} fusion(bf16[1024,256]{1,0:T(8,128)(2,1)} %get-tuple-element.4, bf16[256,1024]{1,0:T(8,128)(2,1)S(1)} %copy-done), kind=kOutput, calls=%fused_computation | convolution fusion | flops 537919488 | bytes 3145728 | tf_op jit(solution)/shard_map/dot_general | solution.py:414
  81.5 0.0 copy-done.1
  81.5 0.6 copy.8
Async XLA Ops:
  0.6 77.7 %copy-start = (bf16[256,1024]{1,0:T(8,128)(2,1)S(1)}, bf16[256,1024]{1,0:T(8,128)(2,1)}, u32[]{:S(2)}) copy-start(bf16[256,1024]{1,0:T(8,128)(2,1)} %param.9) | copy-start | bytes 1572868
  78.4 3.1 %copy-start.1 = (f32[2,128]{1,0:T(2,128)S(1)}, f32[2,128]{1,0:T(2,128)}, u32[]{:S(2)}) copy-start(f32[2,128]{1,0:T(2,128)} %get-tuple-element.5) | copy-start | bytes 3076

commit v3 on v1

v3 whole, which is shorter than its diff:
```python
import functools

import jax
import jax.numpy as jnp
from jax import lax
from jax.experimental import pallas as pl
from jax.experimental.pallas import tpu as pltpu
from jax.sharding import PartitionSpec as P

CL_DEV = 2
CAP = 1024
QUARTERS = 4
EMPTY = 2.0**100
LOW = -1e30

norm_eps = 1e-06
MESH = pl.DeviceIdType.MESH


def dot_t(a, b):
    return lax.dot_general(a, b, (((1,), (1,)), ((), ())), preferred_element_type=jnp.float32)


def unit_rows(values):
    return values * lax.rsqrt(jnp.mean(values * values, axis=-1, keepdims=True) + norm_eps)


def slots_of(ids, clusters, send):
    tokens = ids.shape[1]
    step = min(256, tokens)
    names = lax.broadcasted_iota(jnp.int32, (clusters, step), 0)
    before = lax.broadcasted_iota(jnp.int32, (step, step), 0)
    after = lax.broadcasted_iota(jnp.int32, (step, step), 1)
    earlier = jnp.where(before < after, 1.0, 0.0).astype(jnp.bfloat16)
    carry = jnp.zeros((clusters, 1), jnp.float32)
    out = []
    for start in range(0, tokens, step):
        part = ids[:, start : start + step]
        named = jnp.where(names == part, 1.0, 0.0)
        count = jnp.dot(named.astype(jnp.bfloat16), earlier, preferred_element_type=jnp.float32)
        rank = jnp.sum(named * (count + carry), axis=0, keepdims=True)
        carry = carry + jnp.sum(named, axis=1, keepdims=True)
        out.append(part * send + rank.astype(jnp.int32))
    return jnp.concatenate(out, axis=1)


def kernel(n, heads, send, q_hbm, k_hbm, v_hbm, ids_ref, joined_ref, cent_ref,
           rows, msg, recv, att, back, others, keys, bias, idx, cols,
           in_sem, f_send, f_recv, b_send, b_recv, h_send, h_recv, i_send, i_recv):
    tokens, width = q_hbm.shape[1], q_hbm.shape[2]
    clusters = CL_DEV * n
    part = n // QUARTERS
    block = part * send
    me = lax.axis_index("ctx")
    head = lax.axis_index("head")
    zone = me // part

    loads = []
    for i, ref in enumerate((q_hbm, k_hbm, v_hbm)):
        load = pltpu.make_async_copy(ref.at[0], rows.at[:, i * width : (i + 1) * width], in_sem.at[i])
        load.start()
        loads.append(load)

    barrier = pltpu.get_barrier_semaphore()

    def greet(i, carry):
        pl.semaphore_signal(barrier, inc=1, device_id=(lax.rem(me + i, n), head), device_id_type=MESH)
        return carry

    lax.fori_loop(1, n, greet, 0)
    for i in range(1, heads):
        pl.semaphore_signal(barrier, inc=1, device_id=(me, lax.rem(head + i, heads)), device_id_type=MESH)

    def column(slot_row):
        return jnp.transpose(jnp.broadcast_to(slot_row, (128, tokens)))

    slot_row = slots_of(ids_ref[...], clusters, send)
    cols[0] = column(slot_row)
    rows[:, 3 * width :] = jnp.ones((tokens, width), jnp.bfloat16)
    for load in loads:
        load.wait()

    place_r = lax.broadcasted_iota(jnp.int32, (block, tokens), 0)
    place_r = place_r + (place_r // send) * ((CL_DEV - 1) * send)

    def fill(j, z):
        base = (z * part * CL_DEV + j) * send
        place = jnp.where(place_r + base == slot_row, 1.0, 0.0).astype(jnp.bfloat16)
        placed = jnp.dot(place, rows[...], preferred_element_type=jnp.float32)
        held = placed[:, 3 * width :]
        new = jnp.concatenate(
            [
                placed[:, :width],
                jnp.where(held > 0.5, placed[:, width : 2 * width], EMPTY),
                placed[:, 2 * width : 3 * width],
            ],
            axis=1,
        ).astype(jnp.bfloat16)
        msg[j, pl.ds(z * part, part)] = new.reshape(part, send, 3 * width)

    def forward(j, d, source):
        return pltpu.make_async_remote_copy(
            src_ref=msg.at[j, d], dst_ref=recv.at[j, source], send_sem=f_send.at[j, d], recv_sem=f_recv.at[j, source],
            device_id=(d, head), device_id_type=MESH)

    def ship(j, z):
        def one(i, carry):
            d = z * part + lax.rem(me + i, part)

            @pl.when(d != me)
            def _():
                forward(j, d, me).start()

            return carry

        lax.fori_loop(0, part, one, 0)

    def turn(t):
        return t // QUARTERS, lax.rem(zone + QUARTERS // 2 + lax.rem(t, QUARTERS), QUARTERS)

    def told(i):
        return pltpu.make_async_remote_copy(
            src_ref=ids_ref, dst_ref=idx.at[i - 1], send_sem=i_send.at[i - 1], recv_sem=i_recv.at[i - 1],
            device_id=(me, lax.rem(head + i, heads)), device_id_type=MESH)

    fill(*turn(0))
    pl.semaphore_wait(barrier, n - 1 + heads - 1)

    def dispatch(t, carry):
        fill(*turn(t))
        ship(*turn(t - 1))
        return carry

    steps = CL_DEV * QUARTERS
    lax.fori_loop(1, steps, dispatch, 0)
    ship(*turn(steps - 1))
    for j in range(CL_DEV):
        recv[j, me] = msg[j, me]
    for i in range(1, heads):
        told(i).start()
    for i in range(1, heads):
        told(i).wait_recv()
        cols[i] = column(slots_of(idx[i - 1], clusters, send))

    def arrived(j, z):
        def one(s, carry):
            @pl.when(s != me)
            def _():
                forward(j, s, s).wait_recv()

            return carry

        lax.fori_loop(z * part, (z + 1) * part, one, 0)

    def returned(j, s, owner):
        return pltpu.make_async_remote_copy(
            src_ref=att.at[j, s], dst_ref=back.at[j, owner], send_sem=b_send.at[j, s], recv_sem=b_recv.at[j, owner],
            device_id=(s, head), device_id_type=MESH)

    tri_r = lax.broadcasted_iota(jnp.int32, (block, block), 0)
    tri_c = lax.broadcasted_iota(jnp.int32, (block, block), 1)
    causal = jnp.where(tri_c <= tri_r, 0.0, LOW)
    ones = jnp.ones((8, width), jnp.bfloat16)
    scale = jnp.float32(width ** (-0.5))

    for j in range(CL_DEV):
        sums = jnp.zeros((1, width), jnp.float32)
        for b in range(QUARTERS):
            first, last, span = b * part, (b + 1) * part, (b + 1) * block
            arrived(j, b)
            q = recv[j, first:last, :, :width].reshape(block, width)
            k32 = recv[j, first:last, :, width : 2 * width].reshape(block, width).astype(jnp.float32)
            vacant = k32 > 0.5 * EMPTY
            k32 = jnp.where(vacant, 0.0, k32)
            keys[b * block : span, :] = k32.astype(jnp.bfloat16)
            flags = dot_t(ones, jnp.where(vacant, 1.0, 0.0).astype(jnp.bfloat16))
            bias[:, b * block : span] = jnp.where(flags > 0.5, LOW, 0.0)
            scores = dot_t(q, keys[:span, :]) * scale + bias[0:1, :span]
            tail = scores[:, b * block :] + causal
            scores = tail if b == 0 else jnp.concatenate([scores[:, : b * block], tail], axis=1)
            highest = jnp.max(scores, axis=1, keepdims=True)
            weights = jnp.exp(scores - highest)
            total = jnp.sum(weights, axis=1, keepdims=True)
            v = recv[j, :last, :, 2 * width :].reshape(span, width)
            mixed = jnp.dot(weights.astype(jnp.bfloat16), v, preferred_element_type=jnp.float32)
            att[j, first:last] = (mixed / total).astype(jnp.bfloat16).reshape(part, send, width)
            unit = unit_rows(q.astype(jnp.float32)) + unit_rows(k32)
            sums = sums + jnp.sum(unit, axis=0, keepdims=True)

            def give(s, carry):
                @pl.when(s != me)
                def _():
                    returned(j, s, me).start()

                return carry

            lax.fori_loop(first, last, give, 0)
        back[j, me] = att[j, me]
        mean = jnp.mean(sums * sums, axis=-1, keepdims=True)
        cent_ref[j : j + 1, :] = sums * lax.rsqrt(mean + norm_eps)

    lanes = lax.broadcasted_iota(jnp.int32, (tokens, block), 1)
    lanes = lanes + (lanes // send) * ((CL_DEV - 1) * send)

    def gather(got, which, j, b, piece):
        column_slots = cols[which]
        wide = column_slots if block == 128 else jnp.concatenate([column_slots] * (block // 128), axis=1)
        pick = jnp.where(wide == lanes + (b * part * CL_DEV + j) * send, 1.0, 0.0).astype(jnp.bfloat16)
        return got + jnp.dot(pick, piece.reshape(block, width), preferred_element_type=jnp.float32)

    def passed(i, j, b):
        rows_of = slice(b * part, (b + 1) * part)
        return pltpu.make_async_remote_copy(
            src_ref=back.at[j, rows_of], dst_ref=others.at[i - 1, j, rows_of],
            send_sem=h_send.at[i - 1, j, b], recv_sem=h_recv.at[i - 1, j, b],
            device_id=(me, lax.rem(head + i, heads)), device_id_type=MESH)

    pieces = [(j, b) for j in range(CL_DEV) for b in range(QUARTERS)]
    got = jnp.zeros((tokens, width), jnp.float32)
    for j, b in pieces:

        def wait_back(s, carry):
            @pl.when(s != me)
            def _():
                returned(j, s, s).wait_recv()

            return carry

        lax.fori_loop(b * part, (b + 1) * part, wait_back, 0)
        for i in range(1, heads):
            passed(i, j, b).start()
        got = gather(got, 0, j, b, back[j, b * part : (b + 1) * part])
    joined_ref[:, pl.ds(pl.multiple_of(head * width, width), width)] = got.astype(jnp.bfloat16)

    for i in range(1, heads):
        got = jnp.zeros((tokens, width), jnp.float32)
        for j, b in pieces:
            passed(i, j, b).wait_recv()
            got = gather(got, i, j, b, others[i - 1, j, b * part : (b + 1) * part])
        source = lax.rem(head + heads - i, heads)
        joined_ref[:, pl.ds(pl.multiple_of(source * width, width), width)] = got.astype(jnp.bfloat16)

    def settle(i, carry):
        d = lax.rem(me + i, n)
        for j in range(CL_DEV):
            forward(j, d, me).wait_send()
            returned(j, d, me).wait_send()
        return carry

    lax.fori_loop(1, n, settle, 0)
    for i in range(1, heads):
        told(i).wait_send()
        for j, b in pieces:
            passed(i, j, b).wait_send()


def shards(n, heads, queries, key_rows, value_rows, cluster_ids, out_weight):
    tokens, width = queries.shape[1], queries.shape[2]
    send = CAP // n
    bf16, f32 = jnp.bfloat16, jnp.float32
    dma = pltpu.SemaphoreType.DMA
    joined, centroids = pl.pallas_call(
        functools.partial(kernel, n, heads, send),
        out_shape=(
            jax.ShapeDtypeStruct((tokens, heads * width), bf16),
            jax.ShapeDtypeStruct((CL_DEV, width), f32),
        ),
        in_specs=[pl.BlockSpec(memory_space=pltpu.HBM)] * 3 + [pl.BlockSpec(memory_space=pltpu.VMEM)],
        out_specs=(pl.BlockSpec(memory_space=pltpu.VMEM), pl.BlockSpec(memory_space=pltpu.VMEM)),
        scratch_shapes=[
            pltpu.VMEM((tokens, 4 * width), bf16),
            pltpu.VMEM((CL_DEV, n, send, 3 * width), bf16),
            pltpu.VMEM((CL_DEV, n, send, 3 * width), bf16),
            pltpu.VMEM((CL_DEV, n, send, width), bf16),
            pltpu.VMEM((CL_DEV, n, send, width), bf16),
            pltpu.VMEM((max(1, heads - 1), CL_DEV, n, send, width), bf16),
            pltpu.VMEM((CAP, width), bf16),
            pltpu.VMEM((8, CAP), f32),
            pltpu.VMEM((max(1, heads - 1), 1, tokens), jnp.int32),
            pltpu.VMEM((heads, tokens, 128), jnp.int32),
            dma((3,)),
            dma((CL_DEV, n)),
            dma((CL_DEV, n)),
            dma((CL_DEV, n)),
            dma((CL_DEV, n)),
            dma((max(1, heads - 1), CL_DEV, QUARTERS)),
            dma((max(1, heads - 1), CL_DEV, QUARTERS)),
            dma((max(1, heads - 1),)),
            dma((max(1, heads - 1),)),
        ],
        compiler_params=pltpu.CompilerParams(
            collective_id=0, has_side_effects=True, vmem_limit_bytes=60000000
        ),
        name="route",
    )(queries, key_rows, value_rows, cluster_ids[0, :, 0][None, :])
    projected = jnp.dot(joined, out_weight, preferred_element_type=f32).astype(bf16)
    return (projected, centroids[None])


def solution(mesh):
    in_specs = (
        P("head", "ctx", None),
        P("head", "ctx", None),
        P("head", "ctx", None),
        P("head", "ctx", None),
        P(None, "head"),
    )
    out_specs = (P("ctx", "head"), P("head", "ctx", None))
    body = functools.partial(shards, mesh.shape["ctx"], mesh.shape["head"])
    return jax.shard_map(body, mesh=mesh, in_specs=in_specs, out_specs=out_specs, check_vma=False)
```

time: 69.7 us -> 68.6 us (0.984); the launches traced: 69.5 us -> 67.6 us
  local copies, waits for them, and re-layouts: 4.16 us -> 0.58 us
  matrix products: 2.04 us -> 3.08 us
  Pallas kernels: 62.6 us -> 63.3 us
    unnamed x11 -> x5, local copies, waits for them, and re-layouts: 4.16 us -> 0.58 us
    dot_general x1, matrix products: 2.04 us -> 3.08 us  [shards(): jnp.dot(joined, out_weight, preferred_element_type=f32).astype(bf16)]
    pallas_call x1, Pallas kernels: 62.6 us -> 63.3 us  [shards(): pl.pallas_call(functools.partial(kernel, n, heads, send), out_shape=(jax....]
where the time goes in v3:
time: 68.6 us; the launch traced here: 67.6 us
  Pallas kernels  63.3 us (92%)
  matrix products  3.08 us (4%)
    pallas_call x1, Pallas kernels, shards(): pl.pallas_call(functools.partial(kernel, n, heads, send), out_shape=(jax....  63.3 us
    dot_general x1, matrix products, shards(): jnp.dot(joined, out_weight, preferred_element_type=f32).astype(bf16)  3.08 us

profile of v3, /device:TPU:26, one launch (start us, length us, event | category | flops | bytes accessed | tf_op | source)
XLA Modules:
  0.0 67.6 jit_solution(9520155990003464466)
XLA Ops:
  0.6 0.0 copy-start
  0.6 63.3 %route.1 = (bf16[1024,256]{1,0:T(8,128)(2,1)}, f32[2,128]{1,0:T(2,128)}) custom-call(bf16[1,1024,128]{2,1,0:T(8,128)(2,1)} %q_hbm.1, bf16[1,1024,128]{2,1,0:T(8,128)(2,1)} %k_hbm.1, bf16[1,1024,128]{2,1,0:T(8,128)(2,1)} %v_hbm.1, s32[1,1024]{1,0:T(1,128)} %bitcast.4), custom_call_target="tpu_custom_call" | custom-call | tf_op jit(solution)/shard_map/route/pallas_call | solution.py:262
  64.0 0.0 copy-start.1
  64.0 0.0 copy-done
  64.0 3.1 %convolution_convert_fusion = bf16[1024,1024]{1,0:T(8,128)(2,1)} fusion(bf16[1024,256]{1,0:T(8,128)(2,1)} %get-tuple-element.4, bf16[256,1024]{1,0:T(8,128)(2,1)S(1)} %copy-done), kind=kOutput, calls=%fused_computation | convolution fusion | flops 537919488 | bytes 3145728 | tf_op jit(solution)/shard_map/dot_general | solution.py:296
  67.1 0.0 copy-done.1
  67.1 0.6 copy.8
Async XLA Ops:
  0.6 63.4 %copy-start = (bf16[256,1024]{1,0:T(8,128)(2,1)S(1)}, bf16[256,1024]{1,0:T(8,128)(2,1)}, u32[]{:S(2)}) copy-start(bf16[256,1024]{1,0:T(8,128)(2,1)} %param.9) | copy-start | bytes 1572868
  64.0 3.1 %copy-start.1 = (f32[2,128]{1,0:T(2,128)S(1)}, f32[2,128]{1,0:T(2,128)}, u32[]{:S(2)}) copy-start(f32[2,128]{1,0:T(2,128)} %get-tuple-element.5) | copy-start | bytes 3076

commit v4 on v1

--- a/solution.py
+++ b/solution.py
@@ -106,8 +106,12 @@
             def _():
                 forward(d).start()
 
-    half = chunks // 2
-    order = lambda i: lax.rem(mine + half + i, chunks)
+    quarter = chunks // 4
+
+    def order(i):
+        turn = lax.rem(i + 1, chunks)
+        return lax.rem(mine // quarter + turn // quarter, 4) * quarter + lax.rem(mine + turn, quarter)
+
     fill(order(0))
     pl.semaphore_wait(barrier, n - 1 + heads - 1)
 
@@ -267,7 +271,7 @@
             dma((max(1, heads - 1),)),
         ],
         compiler_params=pltpu.CompilerParams(
-            collective_id=0, has_side_effects=True, vmem_limit_bytes=48 * 1024 * 1024
+            collective_id=0, has_side_effects=True, vmem_limit_bytes=60000000
         ),
         name="route",
     )(queries, key_rows, value_rows, cluster_ids[0, :, 0][None, :])

time: 69.7 us -> 69.3 us (level)
  the two profiles are of different devices: /device:TPU:26 before, /device:TPU:18 now
where the time goes in v4:
time: 69.3 us; the launch traced here: 69.2 us
  Pallas kernels  64.8 us (94%)
  matrix products  3.08 us (4%)
    pallas_call x1, Pallas kernels, shards(): pl.pallas_call(functools.partial(kernel, n, heads, send), out_shape=(jax....  64.8 us
    dot_general x1, matrix products, shards(): jnp.dot(joined, out_weight, preferred_element_type=f32).astype(bf16)  3.08 us

profile of v4, /device:TPU:18, one launch (start us, length us, event | category | flops | bytes accessed | tf_op | source)
XLA Modules:
  0.0 69.2 jit_solution(14401842611126999917)
XLA Ops:
  0.6 0.0 copy-start
  0.6 64.8 %route.1 = (bf16[1024,256]{1,0:T(8,128)(2,1)}, f32[2,128]{1,0:T(2,128)}) custom-call(bf16[1,1024,128]{2,1,0:T(8,128)(2,1)} %q_hbm.1, bf16[1,1024,128]{2,1,0:T(8,128)(2,1)} %k_hbm.1, bf16[1,1024,128]{2,1,0:T(8,128)(2,1)} %v_hbm.1, s32[1,1024]{1,0:T(1,128)} %bitcast.4), custom_call_target="tpu_custom_call" | custom-call | tf_op jit(solution)/shard_map/route/pallas_call | solution.py:249
  65.5 0.0 copy-start.1
  65.5 0.0 copy-done
  65.5 3.1 %convolution_convert_fusion = bf16[1024,1024]{1,0:T(8,128)(2,1)} fusion(bf16[1024,256]{1,0:T(8,128)(2,1)} %get-tuple-element.4, bf16[256,1024]{1,0:T(8,128)(2,1)S(1)} %copy-done), kind=kOutput, calls=%fused_computation | convolution fusion | flops 537919488 | bytes 3145728 | tf_op jit(solution)/shard_map/dot_general | solution.py:278
  68.6 0.0 copy-done.1
  68.6 0.6 copy.8
Async XLA Ops:
  0.6 64.9 %copy-start = (bf16[256,1024]{1,0:T(8,128)(2,1)S(1)}, bf16[256,1024]{1,0:T(8,128)(2,1)}, u32[]{:S(2)}) copy-start(bf16[256,1024]{1,0:T(8,128)(2,1)} %param.9) | copy-start | bytes 1572868
  65.5 3.1 %copy-start.1 = (f32[2,128]{1,0:T(2,128)S(1)}, f32[2,128]{1,0:T(2,128)}, u32[]{:S(2)}) copy-start(f32[2,128]{1,0:T(2,128)} %get-tuple-element.5) | copy-start | bytes 3076
